TPU v7x, 512 devices: a whole 4x8x8 slice. The times are simulated.
512 devices in a mesh: dp: 16 (over z, core), ctx: 8 (over x, y_lo), mp: 4 (over y_hi).
Axes of the slice: x: 4, y: 8 (y_hi: 4, y_lo: 2; y = y_hi * 2 + y_lo), z: 8, core: 2. Of those that a mesh axis runs over, the one named last changes fastest.
Arguments:
- queries: bfloat16 [16, 1024, 4096], P('dp', 'ctx', 'mp'), may hold values from -1.6953125 to 1.6953125
- keys: bfloat16 [16, 1024, 4096], P('dp', 'ctx', 'mp'), may hold values from -1.6953125 to 1.6953125
- values: bfloat16 [16, 1024, 4096], P('dp', 'ctx', 'mp'), may hold values from -6 to 6
- cross_queries: bfloat16 [16, 1024, 4096], P('dp', 'ctx', 'mp'), may hold values from -1.6953125 to 1.6953125
- encoded_bank: bfloat16 [16, 64, 64, 896], P('dp', 'ctx'), may hold values from -6 to 6
- key_weight: bfloat16 [896, 4096], P(('dp', 'ctx'), 'mp'), may hold values from -0.1875 to 0.1875
- value_weight: bfloat16 [896, 4096], P(('dp', 'ctx'), 'mp'), may hold values from -0.1875 to 0.1875
- owner_ids: int32 [16, 16, 2], P('dp', 'ctx'), may hold values from 0 to 15, as said below
- unit_ids: int32 [16, 16, 2], P('dp', 'ctx'), may hold values from 0 to 6
- lengths: int32 [16], P('dp'), may hold values from 64 to 1024
Outputs:
- self_core: bfloat16 [16, 1024, 4096], P('dp', 'ctx', 'mp')
- cross_core: bfloat16 [16, 1024, 4096], P('dp', 'ctx', 'mp')
Inputs may be any that keep to these rules, and one draw needn't show every extreme that they name: `owner_ids`: among the 4 neighbours of the spans of one device (aligned blocks of 2 spans), no owner is named more than once.
All inputs are finite; a program needn't handle non-finite values.
Results may differ from a plain program's by a relative error of at most 0.006.
Values may be sent and summed in bfloat16 or wider, within the bound.
No kernel may reach another device: no remote copies, remote signals or barrier semaphores. Data moves between devices by JAX's collectives and lax.ppermute only.
A program may use at most 64 MiB of HBM per device.

v0:
```python
import math
import jax
import jax.numpy as jnp
from jax import lax
from jax.sharding import PartitionSpec as P

HD = 128
SPAN = 64
NBR = 2


def attend_block(totals, query_heads, positions, key_piece, value_piece, start):
    key_count = key_piece.shape[0]
    head_count = query_heads.shape[1]
    key_heads = key_piece.reshape(key_count, head_count, HD)
    value_heads = value_piece.reshape(key_count, head_count, HD)
    block_size = 512
    last_position = positions[-1]
    for offset in range(0, key_count, block_size):
        key_block = key_heads[offset : offset + block_size]
        value_block = value_heads[offset : offset + block_size]
        block_start = start + offset

        def compute(current):
            running_sums, running_totals = current
            scores = jnp.einsum(
                "qhd,khd->hqk", query_heads, key_block, preferred_element_type=jnp.float32
            ) * (1.0 / math.sqrt(HD))
            key_pos = block_start + jnp.arange(block_size, dtype=jnp.int32)
            allowed = key_pos[None, :] <= positions[:, None]
            weights = jnp.where(allowed[None], jnp.exp(scores), 0.0)
            running_sums = running_sums + jnp.einsum(
                "hqk,khd->qhd",
                weights.astype(jnp.bfloat16),
                value_block,
                preferred_element_type=jnp.float32,
            )
            running_totals = running_totals + jnp.transpose(jnp.sum(weights, axis=2))
            return (running_sums, running_totals)

        def keep(current):
            return current

        active = jnp.logical_and(True, block_start <= last_position)
        totals = lax.cond(active, compute, keep, totals)
    return totals


def empty_totals(row_count, head_count):
    return (
        jnp.zeros((row_count, head_count, HD), jnp.float32),
        jnp.zeros((row_count, head_count), jnp.float32),
    )


def local(
    queries,
    keys,
    values,
    cross_queries,
    encoded_bank,
    key_weight,
    value_weight,
    owner_ids,
    unit_ids,
    lengths,
):
    tok_rows = queries.shape[1]
    feature_width = queries.shape[2]
    head_count = feature_width // HD
    span_count = tok_rows // SPAN
    ctx_index = lax.axis_index("ctx")
    dossier_length = lengths[0]
    positions = ctx_index * tok_rows + jnp.arange(tok_rows, dtype=jnp.int32)
    live_rows = positions < dossier_length
    query_heads = queries[0].reshape(tok_rows, head_count, HD)
    totals = attend_block(
        empty_totals(tok_rows, head_count),
        query_heads,
        positions,
        lax.all_gather(keys, "ctx", axis=1, tiled=True)[0],
        lax.all_gather(values, "ctx", axis=1, tiled=True)[0],
        jnp.int32(0),
    )
    self_heads = totals[0] / totals[1][:, :, None]
    self_core = (
        jnp.where(live_rows[:, None, None], self_heads, 0.0)
        .astype(jnp.bfloat16)
        .reshape(1, tok_rows, feature_width)
    )
    dp_count = lax.axis_size("dp")
    request_total = span_count * NBR
    capacity = -(-request_total // dp_count)
    owners_flat = owner_ids[0].reshape(request_total)
    units_flat = unit_ids[0].reshape(request_total)
    request_order = jnp.arange(request_total, dtype=jnp.int32)
    span_starts = positions[::SPAN]
    live_request = jnp.repeat(span_starts < dossier_length, NBR)
    same_owner = (owners_flat[None, :] == owners_flat[:, None]) & (
        request_order[None, :] < request_order[:, None]
    )
    rank_index = jnp.sum(same_owner.astype(jnp.int32), axis=1)
    slot_index = owners_flat * capacity + rank_index
    slot_numbers = jnp.arange(dp_count * capacity, dtype=jnp.int32)
    matches = (slot_index[:, None] == slot_numbers[None, :]) & live_request[:, None]
    requests = (jnp.sum(jnp.where(matches, units_flat[:, None] + 1, 0), axis=0) - 1).reshape(
        dp_count, capacity
    )
    enc_width = encoded_bank.shape[3]
    bank_local = encoded_bank[0]
    unit_total = bank_local.shape[0]
    asked_units = lax.all_to_all(requests, "dp", split_axis=0, concat_axis=0, tiled=True)
    present = asked_units >= 0
    leading = jnp.clip(asked_units, 0, unit_total - 2)
    joined = jnp.concatenate(
        (jnp.take(bank_local, leading, axis=0), jnp.take(bank_local, leading + 1, axis=0)), axis=2
    )
    joined = jnp.where(present[:, :, None, None], joined, jnp.zeros_like(joined))
    received = lax.all_to_all(joined, "dp", split_axis=0, concat_axis=0, tiled=True)
    own_rows = jnp.take(
        received.reshape(dp_count * capacity, 2 * SPAN, enc_width), slot_index, axis=0
    )
    full_key_weight, full_value_weight = (
        lax.all_gather(key_weight, ("dp", "ctx"), axis=0, tiled=True),
        lax.all_gather(value_weight, ("dp", "ctx"), axis=0, tiled=True),
    )
    retrieved = own_rows.reshape(request_total * 2 * SPAN, enc_width)
    key_proj = jnp.dot(retrieved, full_key_weight, preferred_element_type=jnp.float32).reshape(
        span_count, NBR * 2 * SPAN, head_count, HD
    )
    key_scale = lax.rsqrt(jnp.mean(key_proj * key_proj, axis=3, keepdims=True) + 1e-06)
    cross_keys = (key_proj * key_scale).astype(jnp.bfloat16)
    cross_values = (
        jnp.dot(retrieved, full_value_weight, preferred_element_type=jnp.float32)
        .astype(jnp.bfloat16)
        .reshape(span_count, NBR * 2 * SPAN, head_count, HD)
    )
    span_queries = cross_queries[0].reshape(span_count, SPAN, head_count, HD)
    cross_scores = jnp.einsum(
        "cqhd,ckhd->chqk", span_queries, cross_keys, preferred_element_type=jnp.float32
    ) * (1.0 / math.sqrt(HD))
    cross_weights = jnp.exp(cross_scores)
    cross_sums = jnp.einsum(
        "chqk,ckhd->cqhd",
        cross_weights.astype(jnp.bfloat16),
        cross_values,
        preferred_element_type=jnp.float32,
    )
    cross_totals = jnp.transpose(jnp.sum(cross_weights, axis=3), (0, 2, 1))
    cross_heads = (cross_sums / cross_totals[:, :, :, None]).reshape(tok_rows, head_count, HD)
    cross_core = (
        jnp.where(live_rows[:, None, None], cross_heads, 0.0)
        .astype(jnp.bfloat16)
        .reshape(1, tok_rows, feature_width)
    )
    return (self_core, cross_core)


def solution(mesh):
    in_specs = (
        P("dp", "ctx", "mp"),
        P("dp", "ctx", "mp"),
        P("dp", "ctx", "mp"),
        P("dp", "ctx", "mp"),
        P("dp", "ctx", None, None),
        P(("dp", "ctx"), "mp"),
        P(("dp", "ctx"), "mp"),
        P("dp", "ctx", None),
        P("dp", "ctx", None),
        P("dp"),
    )
    out_specs = (P("dp", "ctx", "mp"), P("dp", "ctx", "mp"))
    return jax.shard_map(local, mesh=mesh, in_specs=in_specs, out_specs=out_specs, check_vma=False)
```

profile of v0, /device:TPU:6, one launch (start us, length us, event | category | flops | bytes accessed | tf_op | source)
XLA Modules:
  0.0 928.9 jit_solution(18198151895259171869)
XLA Ops:
  7.2 0.7 all-gather.13.cloned.1.call-update
  8.0 0.7 all-gather.11.cloned.1.call-update
  9.3 0.7 broadcast_add_fusion
  10.1 0.8 reshape_squeeze.16
  11.4 0.7 copy.76
  12.1 10.4 %all-to-all-start = ((s32[16,1,1]{2,1,0:T(1,128)}), s32[16,1,1]{2,1,0:T(1,128)S(1)}, u32[]{:S(2)}, u32[]{:S(2)}) async-start(s32[16,1,1]{2,1,0:T(1,128)} %copy.76), calls=%async_computation | async-start | bytes 16384 | tf_op jit(solution)/shard_map/all_to_all | solution.py:112
  22.6 1.8 copy.69
  24.4 5.7 all-to-all-done
  30.0 0.4 clamp_reduce_fusion
  30.5 0.8 gather_fusion.2
  31.3 1.5 bitcast_select_fusion
  32.8 0.4 compare_reduce_fusion
  33.2 0.9 gather_fusion.1
  34.3 1.2 copy-done.1
  35.6 2.8 maximum_select_fusion
  38.4 4.6 all-to-all-start.1
  43.2 0.9 copy.70
  44.0 0.6 slice.32
  46.1 0.8 copy.68
  47.0 0.5 broadcast_in_dim.132
  47.5 0.7 copy.90
  48.3 0.6 broadcast_bitcast_fusion
  48.9 355.5 %all-gather.13.cloned.1.call-done = bf16[128,7,1024]{2,1,0:T(8,128)(2,1)} async-done(((bf16[1,7,1024]{2,1,0:T(8,128)(2,1)}), bf16[128,7,1024]{2,1,0:T(8,128)(2,1)}) %all-gather.13.cloned.1.call-update) | async-done | bytes 1835024 | tf_op jit(solution)/shard_map/all_gather | solution.py:124
  404.4 2.7 reshape.338
  407.1 2.5 copy.77
  409.6 369.7 %all-gather.11.cloned.1.call-done = bf16[128,7,1024]{2,1,0:T(8,128)(2,1)} async-done(((bf16[1,7,1024]{2,1,0:T(8,128)(2,1)}), bf16[128,7,1024]{2,1,0:T(8,128)(2,1)}) %all-gather.11.cloned.1.call-update) | async-done | bytes 1835024 | tf_op jit(solution)/shard_map/all_gather | solution.py:125
  779.3 3.9 reshape.336
  783.2 61.9 %all-gather.7.cloned.1.call-done = bf16[1,1024,1024]{1,2,0:T(8,128)(2,1)} async-done(((bf16[1,128,1024]{1,2,0:T(8,128)(2,1)}), bf16[1,1024,1024]{1,2,0:T(8,128)(2,1)}) %all-gather.7.cloned.1.call-update) | async-done | bytes 2097168 | tf_op jit(solution)/shard_map/all_gather | solution.py:81
  845.1 58.6 %all-gather.9.cloned.1.call-done = bf16[1,1024,1024]{1,2,0:T(8,128)(2,1)} async-done(((bf16[1,128,1024]{1,2,0:T(8,128)(2,1)}), bf16[1,1024,1024]{1,2,0:T(8,128)(2,1)}) %all-gather.9.cloned.1.call-update) | async-done | bytes 2097168 | tf_op jit(solution)/shard_map/all_gather | solution.py:82
  903.7 1.2 slice-done
  905.0 2.4 conditional.2
  905.1 1.7 fusion
  906.8 0.5 convolution_bitcast_fusion
  907.3 3.4 conditional.3
  907.4 1.4 slice.24
  908.9 0.3 copy-done.2
  909.4 0.7 fusion.8
  910.1 0.6 fusion.10
  911.1 0.8 reshape.303
  911.9 2.7 gather_fusion
  914.9 2.8 fusion.17
  917.7 0.3 copy.91
  918.0 0.3 copy-done.10
  918.5 0.8 copy-done.4
  919.2 1.3 multiply_reduce_fusion
  920.5 0.4 fusion.30
  920.9 0.3 fusion.20
  921.6 0.8 select_convert_fusion
  (63 shorter events, 2.8 us)
Async XLA Ops:
  7.2 23.3 %copy-start = (bf16[1,8,64,896]{3,2,1,0:T(8,128)(2,1)S(1)}, bf16[1,8,64,896]{3,2,1,0:T(8,128)(2,1)}, u32[]{:S(2)}) copy-start(bf16[1,8,64,896]{3,2,1,0:T(8,128)(2,1)} %param.20) | copy-start | bytes 2752516
  7.2 397.3 %all-gather.13.cloned.1.call-start = ((), (), s32[]{:S(2)}) async-start(), calls=%async_computation.5 | async-start | bytes 2113536 | tf_op jit(solution)/shard_map/all_gather | solution.py:124
  7.9 771.4 %all-gather.11.cloned.1.call-start = ((), (), s32[]{:S(2)}) async-start(), calls=%async_computation.4 | async-start | bytes 2113536 | tf_op jit(solution)/shard_map/all_gather | solution.py:125
  12.1 18.0 %all-to-all-start = ((s32[16,1,1]{2,1,0:T(1,128)}), s32[16,1,1]{2,1,0:T(1,128)S(1)}, u32[]{:S(2)}, u32[]{:S(2)}) async-start(s32[16,1,1]{2,1,0:T(1,128)} %copy.76), calls=%async_computation | async-start | bytes 16384 | tf_op jit(solution)/shard_map/all_to_all | solution.py:112
  22.5 822.6 %all-gather.7.cloned.1.call-start = ((), (), s32[]{:S(2)}) async-start(), calls=%async_computation.2 | async-start | bytes 2359296 | tf_op jit(solution)/shard_map/all_gather | solution.py:81
  34.1 1.5 copy-start.1
  38.4 4.7 copy-start.6
  38.4 6.2 copy-start.9
  38.4 7.7 copy-start.7
  38.4 9.1 copy-start.8
  38.4 873.5 %all-to-all-start.1 = ((bf16[16,1,128,896]{3,2,1,0:T(8,128)(2,1)}), bf16[16,1,128,896]{3,2,1,0:T(8,128)(2,1)}, u32[]{:S(2)}, u32[]{:S(2)}) async-start(bf16[16,1,128,896]{3,2,1,0:T(8,128)(2,1)} %maximum_select_fusion), calls=%async_computation.1 | async-start | bytes 7340032 | tf_op jit(solution)/shard_map/all_to_all | solution.py:119
  43.1 860.6 %all-gather.9.cloned.1.call-start = ((), (), s32[]{:S(2)}) async-start(), calls=%async_computation.3 | async-start | bytes 2359296 | tf_op jit(solution)/shard_map/all_gather | solution.py:82
  845.1 58.6 %slice-start.1 = ((bf16[1,1024,1024]{1,2,0:T(8,128)(2,1)}), bf16[1,512,1024]{1,2,0:T(8,128)(2,1)S(1)}, s32[]{:S(2)}) async-start(bf16[1,1024,1024]{1,2,0:T(8,128)(2,1)} %all-gather.7.cloned.1.call-done), calls=%async_computation.7 | async-start | bytes 2097152 | tf_op jit(solution)/shard_map/slice | solution.py:20
  903.7 1.2 slice-start
  907.3 1.9 copy-start.2
  907.3 2.0 copy-start.3
  910.7 4.0 copy-start.11
  917.7 0.6 copy-start.10
  917.7 1.5 copy-start.4
  919.2 1.3 copy-start.5
Sparse Core Ops, SparseCore 0:
  10.1 394.2 all-gather.12
  406.6 372.7 all-gather.10
  781.9 63.1 all-gather.6
  846.9 56.7 all-gather.8
where the time goes:
time: 930 us; the launch traced here: 929 us
  waiting for transfers between devices  853 us (92%)
  local copies, waits for them, and re-layouts  28.4 us (3%)
  between operations  16 us (2%)
  starting transfers between devices  15.2 us (2%)
    all_gather x1, waiting for transfers between devices, local(): lax.all_gather(value_weight, ('dp', 'ctx'), axis=0, tiled=True)  370 us
    all_gather x1, waiting for transfers between devices, local(): lax.all_gather(key_weight, ('dp', 'ctx'), axis=0, tiled=True)  356 us
    all_gather x1, waiting for transfers between devices, local(): lax.all_gather(keys, 'ctx', axis=1, tiled=True)[0]  61.9 us
    all_gather x1, waiting for transfers between devices, local(): lax.all_gather(values, 'ctx', axis=1, tiled=True)[0]  58.6 us
  transfers between devices with their start and end apart: 6, of which 5 were waited for; matrix products, arithmetic and copies ran while one was open for 3% of the time, Pallas kernels for 0%

commit v1 on v0

--- a/solution.py
+++ b/solution.py
@@ -78,7 +78,9 @@
         empty_totals(tok_rows, head_count),
         query_heads,
         positions,
-        lax.all_gather(keys, "ctx", axis=1, tiled=True)[0],
+        jnp.concatenate(
+            lax.all_to_all(jnp.stack([keys] * lax.axis_size("ctx")), "ctx", 0, 0), axis=1
+        )[0],
         lax.all_gather(values, "ctx", axis=1, tiled=True)[0],
         jnp.int32(0),
     )

time: 930 us -> 883 us (0.949)
  waiting for transfers between devices: 853 us -> 781 us
  blocking collectives: 0 us -> 17.8 us
    all_gather x1 -> x0, waiting for transfers between devices: 61.9 us -> none  [local(): lax.all_gather(keys, 'ctx', axis=1, tiled=True)[0]]
    all_gather x1, waiting for transfers between devices: 356 us -> 336 us  [local(): lax.all_gather(key_weight, ('dp', 'ctx'), axis=0, tiled=True)]
    all_to_all x0 -> x1, blocking collectives: none -> 17.8 us  [local(): lax.all_to_all(requests, 'dp', split_axis=0, concat_axis=0, tiled=True)]
  transfers between devices with their start and end apart: 6 -> 5, of which waited for: 5 -> 4; matrix products, arithmetic and copies ran while one was open for 3% -> 5% of each run, Pallas kernels for 0% -> 0%
where the time goes in v1:
time: 883 us; the launch traced here: 882 us
  waiting for transfers between devices  781 us (88%)
  local copies, waits for them, and re-layouts  36 us (4%)
  blocking collectives  17.8 us (2%)
  between operations  15.9 us (2%)
  other arithmetic  12.4 us (1%)
  starting transfers between devices  10.4 us (1%)
    all_gather x1, waiting for transfers between devices, local(): lax.all_gather(value_weight, ('dp', 'ctx'), axis=0, tiled=True)  372 us
    all_gather x1, waiting for transfers between devices, local(): lax.all_gather(key_weight, ('dp', 'ctx'), axis=0, tiled=True)  336 us
    all_gather x1, waiting for transfers between devices, local(): lax.all_gather(values, 'ctx', axis=1, tiled=True)[0]  60.5 us
    all_to_all x1, blocking collectives, local(): lax.all_to_all(requests, 'dp', split_axis=0, concat_axis=0, tiled=True)  17.8 us
  transfers between devices with their start and end apart: 5, of which 4 were waited for; matrix products, arithmetic and copies ran while one was open for 5% of the time, Pallas kernels for 0%

profile of v1, /device:TPU:6, one launch (start us, length us, event | category | flops | bytes accessed | tf_op | source)
XLA Modules:
  0.0 882.2 jit_solution(17974770619590664866)
XLA Ops:
  7.2 0.7 all-gather.10.cloned.1.call-update
  8.6 0.7 broadcast_add_fusion
  9.3 0.8 reshape_squeeze.15
  10.5 0.5 compare_and_fusion.1
  11.3 17.8 %all_to_all.16 = s32[16,1,1]{2,1,0:T(1,128)S(1)} all-to-all(s32[16,1,1]{2,1,0:T(1,128)S(1)} %copy.75), channel_id=1, replica_groups=mesh['dp'=16,'ctx'=8,'mp'=4] {'dp'}, dimensions={0} | all-to-all | bytes 128 | tf_op jit(solution)/shard_map/all_to_all | solution.py:114
  29.1 2.6 stack.2
  31.6 5.8 all-to-all-start
  37.4 0.7 all-gather.8.cloned.1.call-update
  38.2 0.4 clamp_reduce_fusion
  38.6 2.0 gather_fusion.2
  40.6 3.0 bitcast_select_fusion
  43.6 0.4 compare_reduce_fusion
  44.0 2.0 gather_fusion.1
  46.0 1.9 bitcast_select_fusion.1
  48.1 2.8 maximum_select_fusion
  50.9 12.0 %all-to-all-done = bf16[8,1,128,1024]{3,2,1,0:T(8,128)(2,1)S(1)} async-done(((bf16[8,1,128,1024]{3,2,1,0:T(8,128)(2,1)}), bf16[8,1,128,1024]{3,2,1,0:T(8,128)(2,1)S(1)}, u32[]{:S(2)}, u32[]{:S(2)}) %all-to-all-start) | async-done | bytes 2097184 | tf_op jit(solution)/shard_map/all_to_all | solution.py:82
  62.9 4.5 all-to-all-start.2
  67.5 0.8 copy.68
  68.4 0.6 slice.32
  70.4 0.8 copy.67
  71.3 0.5 broadcast_in_dim.132
  71.9 1.7 copy.89
  73.6 0.7 fusion.31
  74.3 1.3 broadcast_bitcast_fusion
  75.5 335.5 %all-gather.10.cloned.1.call-done = bf16[128,7,1024]{2,1,0:T(8,128)(2,1)} async-done(((bf16[1,7,1024]{2,1,0:T(8,128)(2,1)}), bf16[128,7,1024]{2,1,0:T(8,128)(2,1)}) %all-gather.10.cloned.1.call-update) | async-done | bytes 1835024 | tf_op jit(solution)/shard_map/all_gather | solution.py:126
  411.1 3.9 reshape.341
  414.9 3.9 copy.76
  418.8 371.5 %all-gather.8.cloned.1.call-done = bf16[128,7,1024]{2,1,0:T(8,128)(2,1)} async-done(((bf16[1,7,1024]{2,1,0:T(8,128)(2,1)}), bf16[128,7,1024]{2,1,0:T(8,128)(2,1)}) %all-gather.8.cloned.1.call-update) | async-done | bytes 1835024 | tf_op jit(solution)/shard_map/all_gather | solution.py:127
  790.3 3.9 reshape.339
  794.2 1.3 copy.88
  795.5 60.5 %all-gather.6.cloned.1.call-done = bf16[1,1024,1024]{1,2,0:T(8,128)(2,1)} async-done(((bf16[1,128,1024]{1,2,0:T(8,128)(2,1)}), bf16[1,1024,1024]{1,2,0:T(8,128)(2,1)}) %all-gather.6.cloned.1.call-update) | async-done | bytes 2097168 | tf_op jit(solution)/shard_map/all_gather | solution.py:84
  856.0 1.2 slice-done
  857.6 2.4 conditional.2
  857.7 1.8 fusion
  859.5 0.5 convolution_bitcast_fusion
  860.0 3.9 conditional.3
  860.0 1.3 slice.24
  861.8 0.6 copy-done.7
  862.4 0.8 fusion.10
  863.2 0.6 fusion.12
  864.4 0.8 reshape.306
  865.2 2.7 gather_fusion
  868.2 2.8 fusion.21
  871.2 0.3 copy-done.10
  871.8 0.7 copy-done.2
  872.5 1.3 multiply_reduce_fusion
  873.8 0.4 fusion.34
  874.8 0.8 select_convert_fusion
  (62 shorter events, 3.9 us)
Async XLA Ops:
  7.2 31.4 %copy-start = (bf16[1,8,64,896]{3,2,1,0:T(8,128)(2,1)S(1)}, bf16[1,8,64,896]{3,2,1,0:T(8,128)(2,1)}, u32[]{:S(2)}) copy-start(bf16[1,8,64,896]{3,2,1,0:T(8,128)(2,1)} %param.20) | copy-start | bytes 2752516
  7.2 403.9 %all-gather.10.cloned.1.call-start = ((), (), s32[]{:S(2)}) async-start(), calls=%async_computation.5 | async-start | bytes 2113536 | tf_op jit(solution)/shard_map/all_gather | solution.py:126
  10.5 58.5 %copy-start.9 = (s32[4]{0:T(128)}, s32[4]{0:T(128)S(1)}, u32[]{:S(2)}) copy-start(s32[4]{0:T(128)S(1)} %convert_reduce_fusion) | copy-start | bytes 52
  31.6 31.3 %all-to-all-start = ((bf16[8,1,128,1024]{3,2,1,0:T(8,128)(2,1)}), bf16[8,1,128,1024]{3,2,1,0:T(8,128)(2,1)S(1)}, u32[]{:S(2)}, u32[]{:S(2)}) async-start(bf16[8,1,128,1024]{3,2,1,0:T(8,128)(2,1)} %stack.2), calls=%async_computation | async-start | bytes 4194304 | tf_op jit(solution)/shard_map/all_to_all | solution.py:82
  37.4 752.9 %all-gather.8.cloned.1.call-start = ((), (), s32[]{:S(2)}) async-start(), calls=%async_computation.4 | async-start | bytes 2113536 | tf_op jit(solution)/shard_map/all_gather | solution.py:127
  46.0 2.1 copy-start.1
  50.9 16.6 %copy-start.5 = (bf16[1,128,1024]{2,1,0:T(8,128)(2,1)S(1)}, bf16[1,128,1024]{2,1,0:T(8,128)(2,1)}, u32[]{:S(2)}) copy-start(bf16[1,128,1024]{2,1,0:T(8,128)(2,1)} %param.18) | copy-start | bytes 786436
  50.9 18.0 %copy-start.8 = (s32[1,2,2]{2,1,0:T(2,128)S(1)}, s32[1,2,2]{2,1,0:T(2,128)}, u32[]{:S(2)}) copy-start(s32[1,2,2]{2,1,0:T(2,128)} %param.23) | copy-start | bytes 52
  50.9 19.5 %copy-start.6 = (bf16[1,128,1024]{2,1,0:T(8,128)(2,1)S(1)}, bf16[1,128,1024]{2,1,0:T(8,128)(2,1)}, u32[]{:S(2)}) copy-start(bf16[1,128,1024]{2,1,0:T(8,128)(2,1)} %param.16) | copy-start | bytes 786436
  62.9 802.3 %all-to-all-start.2 = ((bf16[16,1,128,896]{3,2,1,0:T(8,128)(2,1)}), bf16[16,1,128,896]{3,2,1,0:T(8,128)(2,1)}, u32[]{:S(2)}, u32[]{:S(2)}) async-start(bf16[16,1,128,896]{3,2,1,0:T(8,128)(2,1)} %maximum_select_fusion), calls=%async_computation.2 | async-start | bytes 7340032 | tf_op jit(solution)/shard_map/all_to_all | solution.py:121
  67.4 788.6 %all-gather.6.cloned.1.call-start = ((), (), s32[]{:S(2)}) async-start(), calls=%async_computation.3 | async-start | bytes 2359296 | tf_op jit(solution)/shard_map/all_gather | solution.py:84
  856.0 1.2 slice-start
  856.0 1.5 copy-start.3
  861.4 1.0 copy-start.7
  863.9 4.0 copy-start.11
  871.0 0.6 copy-start.10
  871.0 1.5 copy-start.2
  872.5 1.3 copy-start.4
Sparse Core Ops, SparseCore 0:
  10.1 400.9 all-gather.9
  413.2 377.0 all-gather.7
  792.9 63.1 all-gather.5
